TPU v7x, 128 devices: a whole 4x4x4 slice. The times are simulated.
128 devices in a mesh: seq: 32 (over y, x, core), head: 4 (over z).
Axes of the slice: x: 4, y: 4, z: 4, core: 2. Of those that a mesh axis runs over, the one named last changes fastest.
Arguments:
- queries: float32 [32768, 8192], P('seq', 'head'), may hold values from -200 to 200, as said below
- keys: float32 [32768, 1024], P('seq', 'head'), may hold values from -8 to 8, as said below
- values: float32 [32768, 1024], P('seq', 'head'), may hold values from -40 to 40, as said below
- gain: float32 [8192], P('head'), may hold values from 0.1 to 1.9
Outputs:
- attended: float32 [32768, 8192], P('seq', 'head')
Inputs may be any that keep to these rules, and one draw needn't show every extreme that they name: `queries`: queries are real-valued. `keys`: keys are real-valued of order one. `values`: values are real-valued; their scale differs between heads.
All inputs are finite; a program needn't handle non-finite values.
Results may differ from a plain program's by a relative error of at most 0.0003.
Values sent between devices are 32-bit elements; how exact they have to be, the bound alone decides.
No kernel may reach another device: no remote copies, remote signals or barrier semaphores. Data moves between devices by JAX's collectives and lax.ppermute only.
A program may use at most 128 MiB of HBM per device.

v0:
```python
import functools
import math

import jax
import jax.numpy as jnp
from jax import lax
from jax.experimental import pallas as pl
from jax.experimental.pallas import tpu as pltpu
from jax.sharding import PartitionSpec as P


QUERY_HEADS = 64
KEY_VALUE_HEADS = 8
D = 128
G = QUERY_HEADS // KEY_VALUE_HEADS
BLOCK = 128
STEP = 2
WIDE = 4
EPS = 1e-6
SCORE_SCALE = math.log2(math.e) / math.sqrt(D)

f32 = jnp.float32
bf = jnp.bfloat16
NT = (((1,), (1,)), ((), ()))
TN = (((0,), (0,)), ((), ()))


def split(x):
    hi = x.astype(bf)
    return hi, (x - hi.astype(f32)).astype(bf)


def lanes(*xs):
    return jnp.concatenate(xs, axis=1)


def rows(*xs):
    return jnp.concatenate(xs, axis=0)


def dot(a, b, dims=(((1,), (0,)), ((), ()))):
    return lax.dot_general(a, b, dims, preferred_element_type=f32)


def halves(x):
    return x[:, :D] + x[:, D:]


def params(mib):
    return pltpu.CompilerParams(
        vmem_limit_bytes=mib << 20, dimension_semantics=("arbitrary",)
    )


def state_body(k_ref, v_ref, before_ref, total_ref, tail_ref, kp_ref, vp_ref):
    count = k_ref.shape[0]
    state = jnp.zeros((D, D), f32)
    for b in range(count // BLOCK):
        at = slice(b * BLOCK, (b + 1) * BLOCK)
        before_ref[b] = state
        k = k_ref[at, :]
        fh, fl = split(jnp.tanh(k))
        vv = lanes(*split(v_ref[at, :]))
        kp_ref[at, :] = lanes(*split(k * SCORE_SCALE), fh, fl)
        vp_ref[at, :] = vv
        state = state + halves(dot(rows(fh, fl), rows(vv, vv), TN))
    total_ref[...] = state
    tail_ref[:BLOCK] = k_ref[count - BLOCK :, :]
    tail_ref[BLOCK:] = v_ref[count - BLOCK :, :]


def local_states(keys, values):
    count, width = keys.shape
    kv, nb = width // D, count // BLOCK
    one = pl.Squeezed()
    whole = lambda *shape: pl.BlockSpec((one, *shape), lambda g: (g,) + (0,) * len(shape))
    return pl.pallas_call(
        state_body,
        grid=(kv,),
        in_specs=[pl.BlockSpec((count, D), lambda g: (0, g))] * 2,
        out_specs=[
            whole(nb, D, D),
            whole(D, D),
            whole(2 * BLOCK, D),
            whole(count, 4 * D),
            whole(count, 2 * D),
        ],
        out_shape=[
            pltpu.VMEM((kv, nb, D, D), f32),
            pltpu.VMEM((kv, D, D), f32),
            pltpu.VMEM((kv, 2 * BLOCK, D), f32),
            pltpu.VMEM((kv, count, 4 * D), bf),
            pltpu.VMEM((kv, count, 2 * D), bf),
        ],
        compiler_params=params(4),
        name="local_states",
    )(keys, values)


def block_copy(piece, q_hbm, q_ref, sems, j):
    to = pl.ds(pl.multiple_of(j * BLOCK, BLOCK), BLOCK)
    at = pl.ds(pl.multiple_of((piece * STEP + j) * BLOCK, BLOCK), BLOCK)
    return pltpu.make_async_copy(q_hbm.at[at], q_ref.at[to], sems.at[j])


def fetch_body(piece, *refs):
    for j in range(STEP):
        block_copy(piece, *refs, j).start()
    for j in range(STEP):
        block_copy(piece, *refs, j).wait()


def first_queries(queries, piece):
    return pl.pallas_call(
        functools.partial(fetch_body, piece),
        in_specs=[pl.BlockSpec(memory_space=pl.ANY)],
        out_specs=pl.BlockSpec(memory_space=pl.ANY),
        out_shape=pltpu.VMEM((STEP * BLOCK, queries.shape[1]), f32),
        scratch_shapes=[pltpu.SemaphoreType.DMA((STEP,))],
        compiler_params=pltpu.CompilerParams(vmem_limit_bytes=2 << 20),
        name="first_queries",
    )(queries)


def place():
    i = lax.axis_index("seq")
    return i // 8, (i // 2) % 4, i % 2


def chip_body(own_ref, other_ref, out_ref):
    core = place()[2]
    out_ref[...] = own_ref[core] + other_ref[core]


def row_body(own_ref, one_ref, two_ref, three_ref, sum_ref, before_ref):
    x = place()[1]
    got = [one_ref[...], two_ref[...], three_ref[...]]
    sum_ref[...] = own_ref[...] + got[0] + got[1] + got[2]
    before = jnp.zeros((D, D), f32)
    for by, state in enumerate(got, 1):
        before = before + jnp.where(x >= by, state, 0.0)
    before_ref[...] = before


def small_call(body, outs, *args):
    shape = jax.ShapeDtypeStruct((D, D), f32)
    return pl.pallas_call(
        body,
        out_shape=[shape] * outs,
        compiler_params=pltpu.CompilerParams(vmem_limit_bytes=2 << 20),
    )(*args)


def block_body(piece, ahead, carried, inner, window, *refs):
    q_ref, kp_ref, vp_ref, *refs = refs
    if piece == 0 and window:
        halo_ref, *refs = refs
    if ahead is not None:
        q_hbm, *refs = refs
    refs = refs[carried:]
    if window:
        win_ref, *refs = refs
    if inner:
        lin_ref, fq_ref, *refs = refs
    kv = kp_ref.shape[0]
    if ahead is not None:
        next_ref, sems = refs
        fetch = functools.partial(block_copy, ahead, q_hbm, next_ref, sems)

        @pl.loop(0, STEP)
        def _(j):
            fetch(j).start()

    row = lax.broadcasted_iota(jnp.int32, (BLOCK, BLOCK), 0)
    col = lax.broadcasted_iota(jnp.int32, (BLOCK, BLOCK), 1)
    own = rows(*[row >= col] * G)
    zero = jnp.zeros((BLOCK * G, BLOCK), bf)

    def in_block(j, g, q, heads, tokens, here):
        fh, fl = kp_ref[g, here, 2 * D : 3 * D], kp_ref[g, here, 3 * D :]
        v_own = vp_ref[g, here, :]
        f2 = lanes(*split(jnp.tanh(q)))
        fq_ref[j, g * G * BLOCK : (g + 1) * G * BLOCK, :] = f2
        ff = rows(lanes(fh, fh), lanes(fl, fl))
        a = jnp.where(own, halves(dot(f2, ff, NT)), 0.0)
        lin = halves(dot(lanes(*split(a)), rows(v_own, v_own)))
        for i, at in enumerate(heads):
            lin_ref[tokens, at] = lin[i * BLOCK : (i + 1) * BLOCK]

    def scores(block, g, q, here, there):
        kh, kl = kp_ref[g, here, :D], kp_ref[g, here, D : 2 * D]
        if block:
            ph, pl_ = kp_ref[g, there, :D], kp_ref[g, there, D : 2 * D]
            v_prior = vp_ref[g, there, :]
        else:
            ph, pl_ = split(halo_ref[g, :BLOCK] * SCORE_SCALE)
            v_prior = lanes(*split(halo_ref[g, BLOCK:]))
        kk = rows(lanes(kh, kh, kl, kl), lanes(ph, ph, pl_, pl_))
        v_both = rows(vp_ref[g, here, :], v_prior)
        qh, ql = split(q)
        return dot(lanes(qh, ql, qh, ql), kk, NT), v_both

    def in_window(block, s, v_both, heads, tokens):
        before = s[:, BLOCK:]
        if block == 0:
            before = jnp.where(lax.axis_index("seq") > 0, before, -1e30)
        t = jnp.where(own, s[:, :BLOCK], before)
        p = jnp.exp2(t - jnp.max(t, axis=1, keepdims=True))
        total = jnp.sum(p, axis=1, keepdims=True)
        wh, wl = split(p)
        p4 = lanes(
            jnp.where(own, wh, zero),
            jnp.where(own, zero, wh),
            jnp.where(own, wl, zero),
            jnp.where(own, zero, wl),
        )
        win = halves(dot(p4, rows(v_both, v_both))) * (1.0 / total)
        for i, at in enumerate(heads):
            win_ref[tokens, at] = win[i * BLOCK : (i + 1) * BLOCK]

    for j in range(STEP):
        block = piece * STEP + j
        tokens = slice(j * BLOCK, (j + 1) * BLOCK)
        here = slice(block * BLOCK, (block + 1) * BLOCK)
        there = slice((block - 1) * BLOCK, block * BLOCK)
        for g in range(kv):
            heads = [slice(i * D, (i + 1) * D) for i in range(g * G, (g + 1) * G)]
            q = rows(*[q_ref[tokens, at] for at in heads])
            if window:
                s, v_both = scores(block, g, q, here, there)
            if inner:
                in_block(j, g, q, heads, tokens, here)
            if window:
                in_window(block, s, v_both, heads, tokens)
    if ahead is not None:
        for j in range(STEP):
            fetch(j).wait()


def block_part(
    piece, q, kp, vp, made, ahead=None, queries=None, halo=None, inner=True, window=True
):
    kv, count, _ = kp.shape
    nb = count // BLOCK
    width = q.shape[1]
    whole = lambda x: pl.BlockSpec(x.shape, lambda _: (0,) * x.ndim)
    args = [q, kp, vp]
    if halo is not None:
        args.append(halo)
    specs = [whole(x) for x in args]
    if ahead is not None:
        args.append(queries)
        specs.append(pl.BlockSpec(memory_space=pl.ANY))
    aliases = {len(args) + i: i for i in range(len(made))}
    big = pl.BlockSpec((STEP * BLOCK, width), lambda _: (piece, 0))
    out_specs, out_shape, scratch = [], [], []
    if window:
        out_specs.append(big)
        out_shape.append(pltpu.VMEM((count, width), f32))
    if inner:
        features = (kv * G * BLOCK, 2 * D)
        out_specs += [big, pl.BlockSpec((STEP, *features), lambda _: (piece, 0, 0))]
        out_shape += [pltpu.VMEM((count, width), f32), pltpu.VMEM((nb, *features), bf)]
    if ahead is not None:
        out_specs.append(pl.BlockSpec(memory_space=pl.ANY))
        out_shape.append(pltpu.VMEM(q.shape, f32))
        scratch.append(pltpu.SemaphoreType.DMA((STEP,)))
    return pl.pallas_call(
        lambda *refs: block_body(piece, ahead, len(made), inner, window, *refs),
        grid=(1,),
        in_specs=specs + [pl.BlockSpec(memory_space=pl.ANY)] * len(made),
        out_specs=out_specs,
        out_shape=out_shape,
        scratch_shapes=scratch,
        input_output_aliases=aliases,
        compiler_params=params(10),
    )(*args, *made)


def linear_body(fq_ref, part_ref, inner_ref, mine_ref, their_ref, other_ref, lin_ref, sq_ref):
    core = place()[2]
    for j in range(WIDE):
        tokens = slice(j * BLOCK, (j + 1) * BLOCK)
        sq = jnp.zeros((BLOCK, D), f32)
        for g in range(other_ref.shape[0]):
            state = jnp.where(core == g, mine_ref[...], their_ref[...])
            state = state + jnp.where(core == 1, other_ref[g], 0.0) + inner_ref[g, j]
            ss = lanes(*split(state))
            fq = fq_ref[j, g * G * BLOCK : (g + 1) * G * BLOCK, :]
            lin = halves(dot(fq, rows(ss, ss)))
            for i in range(G):
                at = slice((g * G + i) * D, (g * G + i + 1) * D)
                x = lin[i * BLOCK : (i + 1) * BLOCK] + part_ref[tokens, at]
                lin_ref[tokens, at] = x
                sq = sq + x * x
        sq_ref[j] = jnp.sum(sq.T, axis=0, keepdims=True)


def linear_part(fq, part, inner, mine, theirs, other):
    count, width = part.shape
    kv, nb = inner.shape[:2]
    big = pl.BlockSpec((WIDE * BLOCK, width), lambda b: (b, 0))
    state = pl.BlockSpec((D, D), lambda b: (0, 0))
    return pl.pallas_call(
        linear_body,
        grid=(nb // WIDE,),
        in_specs=[
            pl.BlockSpec((WIDE,) + fq.shape[1:], lambda b: (b, 0, 0)),
            big,
            pl.BlockSpec((kv, WIDE, D, D), lambda b: (0, b, 0, 0)),
            state,
            state,
            pl.BlockSpec((kv, D, D), lambda b: (0, 0, 0)),
        ],
        out_specs=[big, pl.BlockSpec((WIDE, 1, BLOCK), lambda b: (b, 0, 0))],
        out_shape=[
            pltpu.VMEM((count, width), f32),
            pltpu.VMEM((nb, 1, BLOCK), f32),
        ],
        compiler_params=params(10),
        name="linear",
    )(fq, part, inner, mine, theirs, other)


def combine_body(lin_ref, win_ref, s0, s1, s2, s3, gain_ref, out_hbm, out_ref, sems):
    def send(b):
        row = pl.ds(pl.multiple_of(b * BLOCK, BLOCK), BLOCK)
        return row, pltpu.make_async_copy(out_ref.at[row], out_hbm.at[row], sems.at[b])

    @pl.loop(0, s0.shape[0])
    def _(b):
        ms = ((s0[b] + s1[b]) + (s2[b] + s3[b])) * (1.0 / (QUERY_HEADS * D))
        inv = jnp.broadcast_to(lax.rsqrt(ms + EPS), (BLOCK, BLOCK)).T
        row, copy = send(b)
        for i in range(lin_ref.shape[1] // D):
            at = slice(i * D, (i + 1) * D)
            out_ref[row, at] = lin_ref[row, at] * inv * gain_ref[:, at] + win_ref[row, at]
        copy.start()

    @pl.loop(0, s0.shape[0])
    def _(b):
        send(b)[1].wait()


def combine(lin, win, squares, gain):
    args = [lin, win, *squares, gain]
    return pl.pallas_call(
        combine_body,
        grid=(1,),
        in_specs=[pl.BlockSpec(x.shape, lambda _, x=x: (0,) * x.ndim) for x in args],
        out_specs=pl.BlockSpec(memory_space=pl.ANY),
        out_shape=pltpu.HBM(lin.shape, f32),
        scratch_shapes=[
            pltpu.VMEM(lin.shape, f32),
            pltpu.SemaphoreType.DMA((squares[0].shape[0],)),
        ],
        compiler_params=params(10),
        name="combine",
    )(*args)


def shift_x(by):
    return [(i, i // 8 * 8 + (i + 2 * by) % 8) for i in range(32)]


def down_from(y):
    return [(y * 8 + i, (y + 1) * 8 + i) for i in range(8)]


SWAP = [(i, i ^ 1) for i in range(32)]


def shards(queries, keys, values, gain):
    count = queries.shape[0]
    nb = count // BLOCK
    heads = lax.axis_size("head")
    assert heads == 4 and nb == 8 and lax.axis_size("seq") == 32
    queries, keys, values = (
        pltpu.with_memory_space_constraint(x, pltpu.HBM) for x in (queries, keys, values)
    )

    def move(x, pairs):
        return lax.ppermute(x, "seq", pairs)

    def tie(*xs):
        return lax.optimization_barrier(xs)

    order = (1, 2, 3, 0)
    inner, total, tail, kp, vp = local_states(keys, values)
    other = move(total, SWAP)
    q = first_queries(queries, order[0])
    (chip,) = small_call(chip_body, 1, total, other)
    along_x = [move(chip, shift_x(by)) for by in (1, 2, 3)]
    *made, q = block_part(order[0], q, kp, vp, (), order[1], queries)
    *made, one, two, three = tie(*made, *along_x)
    row, mine = small_call(row_body, 2, chip, one, two, three)
    for y in range(3):
        got = move(row, down_from(y))
        *made, mine = tie(*made, mine)
        if y < 2:
            *made, q = block_part(order[y + 1], q, kp, vp, made, order[y + 2], queries)
        else:
            win, *made = made
            part, fq = block_part(0, q, kp, vp, made, window=False)
            made = [win, part, fq]
        *made, got = tie(*made, got)
        row, mine = row + got, mine + got
    tail, mine = tie(tail, mine)
    theirs = move(mine, SWAP)
    halo = move(tail, [(i, i + 1) for i in range(31)])
    win, part, fq = made
    lin, sq = linear_part(fq, part, inner, mine, theirs, other)
    q, sq = tie(q, sq)
    squares = [sq]
    for by in range(1, heads):
        squares.append(lax.ppermute(sq, "head", [(i, (i + by) % heads) for i in range(heads)]))
    (win,) = block_part(0, q, kp, vp, (win,), halo=halo, inner=False)
    return combine(lin, win, squares, gain[None, :])


def solution(mesh):
    in_specs = (P("seq", "head"), P("seq", "head"), P("seq", "head"), P("head"))
    return jax.shard_map(
        shards, mesh=mesh, in_specs=in_specs, out_specs=P("seq", "head"), check_vma=False
    )
```

profile of v0, /device:TPU:24, one launch (start us, length us, event | category | flops | bytes accessed | tf_op | source)
XLA Modules:
  0.0 49.6 jit_solution(1747838411297188549)
XLA Ops:
  0.0 2.1 %local_states.1 = (f32[2,8,128,128]{3,2,1,0:T(8,128)S(1)}, f32[2,128,128]{2,1,0:T(8,128)S(1)}, f32[2,256,128]{2,1,0:T(8,128)S(1)}, bf16[2,1024,512]{2,1,0:T(8,128)(2,1)S(1)}, bf16[2,1024,256]{2,1,0:T(8,128)(2,1)S(1)}) custom-call(f32[1024,256]{1,0:T(8,128)} %k_ref.1, f32[1024,256]{1,0:T(8,128)} %v_ref.1), custom_call_target="tpu_custom_call" | custom-call | tf_op jit(solution)/shard_map/local_states/pallas_call | solution.py:77
  2.1 0.1 collective-permute-start
  2.2 1.3 %collective-permute-done.other_ref = f32[2,128,128]{2,1,0:T(8,128)S(1)} collective-permute-done((f32[2,128,128]{2,1,0:T(8,128)S(1)}, f32[2,128,128]{2,1,0:T(8,128)S(1)}, u32[]{:S(2)}, u32[]{:S(2)}) %collective-permute-start) | collective-permute-done | bytes 131104 | tf_op jit(solution)/shard_map/ppermute | solution.py:383
  3.5 2.8 %collective-permute-start.3 = (f32[128,128]{1,0:T(8,128)S(1)}, f32[128,128]{1,0:T(8,128)S(1)}, u32[]{:S(2)}, u32[]{:S(2)}) collective-permute-start(f32[128,128]{1,0:T(8,128)S(1)} %shard_map.47.own_ref), channel_id=1, source_target_pairs={{0,24},{4,28},{8,0},{12,4},{16,8},{20,12},{24,16},{28,20},{32,56},... | collective-permute-start | bytes 196616 | tf_op jit(solution)/shard_map/ppermute | solution.py:383
  6.4 0.8 %collective-permute-start.2 = (f32[128,128]{1,0:T(8,128)S(1)}, f32[128,128]{1,0:T(8,128)S(1)}, u32[]{:S(2)}, u32[]{:S(2)}) collective-permute-start(f32[128,128]{1,0:T(8,128)S(1)} %shard_map.47.own_ref), channel_id=1, source_target_pairs={{0,16},{4,20},{8,24},{12,28},{16,0},{20,4},{24,8},{28,12},{32,48},... | collective-permute-start | bytes 196616 | tf_op jit(solution)/shard_map/ppermute | solution.py:383
  7.2 0.9 %collective-permute-start.1 = (f32[128,128]{1,0:T(8,128)S(1)}, f32[128,128]{1,0:T(8,128)S(1)}, u32[]{:S(2)}, u32[]{:S(2)}) collective-permute-start(f32[128,128]{1,0:T(8,128)S(1)} %shard_map.47.own_ref), channel_id=1, source_target_pairs={{0,8},{4,12},{8,16},{12,20},{16,24},{20,28},{24,0},{28,4},{32,40},... | collective-permute-start | bytes 196616 | tf_op jit(solution)/shard_map/ppermute | solution.py:383
  8.1 1.6 %first_queries.1.refs_0_ = f32[256,2048]{1,0:T(8,128)S(1)} custom-call(f32[1024,2048]{1,0:T(8,128)} %refs_3_.5), custom_call_target="tpu_custom_call" | custom-call | tf_op jit(solution)/shard_map/first_queries/pallas_call | solution.py:114
  9.6 3.8 %shard_map.46 = (f32[1024,2048]{1,0:T(8,128)S(1)}, f32[1024,2048]{1,0:T(8,128)S(1)}, bf16[8,2048,256]{2,1,0:T(8,128)(2,1)S(1)}, f32[256,2048]{1,0:T(8,128)S(1)}) custom-call(f32[256,2048]{1,0:T(8,128)S(1)} %first_queries.1.refs_0_, bf16[2,1024,512]{2,1,0:T(8,128)(2,1)S(1)} %get-tuple-element.62.refs_1_, bf16[2,1024,256]{2,1,0:T(8,128)(2,1)S(1)} %get-tuple-element.63.refs_2_, ...), custom_call_target="tpu_custom_call" | custom-call | tf_op jit(solution)/shard_map/pallas_call | solution.py:268
  13.4 0.0 collective-permute-done.3.three_ref
  13.4 0.0 collective-permute-done.2.two_ref
  13.4 0.0 collective-permute-done.1.one_ref
  13.5 0.7 %collective-permute-start.4 = (f32[128,128]{1,0:T(8,128)S(1)}, f32[128,128]{1,0:T(8,128)S(1)}, u32[]{:S(2)}, u32[]{:S(2)}) collective-permute-start(f32[128,128]{1,0:T(8,128)S(1)} %get-tuple-element.83), channel_id=1, source_target_pairs={{0,32},{4,36},{8,40},{12,44},{16,48},{20,52},{24,56},{28,60},{1,33... | collective-permute-start | bytes 196616 | tf_op jit(solution)/shard_map/ppermute | solution.py:383
  14.2 3.8 %shard_map.49 = (f32[1024,2048]{1,0:T(8,128)S(1)}, f32[1024,2048]{1,0:T(8,128)S(1)}, bf16[8,2048,256]{2,1,0:T(8,128)(2,1)S(1)}, f32[256,2048]{1,0:T(8,128)S(1)}) custom-call(f32[256,2048]{1,0:T(8,128)S(1)} %get-tuple-element.64.refs_0_, ...), custom_call_target="tpu_custom_call", output_to_operand_aliasing={{0}: (4, {}), {1}: (5, {}), {2}: (6, {})} | custom-call | tf_op jit(solution)/shard_map/pallas_call | solution.py:268
  17.9 0.0 collective-permute-done.4
  18.0 0.8 %collective-permute-start.5 = (f32[128,128]{1,0:T(8,128)S(1)}, f32[128,128]{1,0:T(8,128)S(1)}, u32[]{:S(2)}, u32[]{:S(2)}) collective-permute-start(f32[128,128]{1,0:T(8,128)S(1)} %get-tuple-element.121), channel_id=1, source_target_pairs={{32,64},{36,68},{40,72},{44,76},{48,80},{52,84},{56,88},{60,92},{3... | collective-permute-start | bytes 196616 | tf_op jit(solution)/shard_map/ppermute | solution.py:383
  18.8 3.8 %shard_map.50 = (f32[1024,2048]{1,0:T(8,128)S(1)}, f32[1024,2048]{1,0:T(8,128)S(1)}, bf16[8,2048,256]{2,1,0:T(8,128)(2,1)S(1)}, f32[256,2048]{1,0:T(8,128)S(1)}) custom-call(f32[256,2048]{1,0:T(8,128)S(1)} %get-tuple-element.79.refs_0_, ...), custom_call_target="tpu_custom_call", output_to_operand_aliasing={{0}: (4, {}), {1}: (5, {}), {2}: (6, {})} | custom-call | tf_op jit(solution)/shard_map/pallas_call | solution.py:268
  22.6 0.0 collective-permute-done.5
  22.6 1.3 %collective-permute-start.6 = (f32[128,128]{1,0:T(8,128)S(1)}, f32[128,128]{1,0:T(8,128)S(1)}, u32[]{:S(2)}, u32[]{:S(2)}) collective-permute-start(f32[128,128]{1,0:T(8,128)S(1)} %get-tuple-element.119), channel_id=1, source_target_pairs={{64,96},{68,100},{72,104},{76,108},{80,112},{84,116},{88,120},{92,... | collective-permute-start | bytes 196616 | tf_op jit(solution)/shard_map/ppermute | solution.py:383
  23.9 1.5 %shard_map.51 = (f32[1024,2048]{1,0:T(8,128)S(1)}, bf16[8,2048,256]{2,1,0:T(8,128)(2,1)S(1)}) custom-call(f32[256,2048]{1,0:T(8,128)S(1)} %get-tuple-element.115.refs_0_, bf16[2,1024,512]{2,1,0:T(8,128)(2,1)S(1)} %get-tuple-element.62.refs_1_, bf16[2,1024,256]{2,1,0:T(8,128)(2,1)S(1)} %get-tuple-element.63.refs_2_, ...), custom_call_target="tpu_custom_call", output_to_operand_aliasing={{0}: (3, {}), {1}: (4, {})} | custom-call | tf_op jit(solution)/shard_map/pallas_call | solution.py:268
  25.5 3.3 %collective-permute-done.6 = f32[128,128]{1,0:T(8,128)S(1)} collective-permute-done((f32[128,128]{1,0:T(8,128)S(1)}, f32[128,128]{1,0:T(8,128)S(1)}, u32[]{:S(2)}, u32[]{:S(2)}) %collective-permute-start.6) | collective-permute-done | bytes 65568 | tf_op jit(solution)/shard_map/ppermute | solution.py:383
  28.8 1.9 %collective-permute-start.8 = (f32[2,256,128]{2,1,0:T(8,128)S(1)}, f32[2,256,128]{2,1,0:T(8,128)S(1)}, u32[]{:S(2)}, u32[]{:S(2)}) collective-permute-start(f32[2,256,128]{2,1,0:T(8,128)S(1)} %get-tuple-element.116), channel_id=1, source_target_pairs={{0,4},{4,8},{8,12},{12,16},{16,20},{20,24},{24,28},{28,32},{32,36}... | collective-permute-start | bytes 786440 | tf_op jit(solution)/shard_map/ppermute | solution.py:383
  30.7 2.0 %collective-permute-start.7 = (f32[128,128]{1,0:T(8,128)S(1)}, f32[128,128]{1,0:T(8,128)S(1)}, u32[]{:S(2)}, u32[]{:S(2)}) collective-permute-start(f32[128,128]{1,0:T(8,128)S(1)} %add.19.mine_ref), channel_id=1, source_target_pairs={{0,4},{4,0},{8,12},{12,8},{16,20},{20,16},{24,28},{28,24},{32,36},... | collective-permute-start | bytes 196616 | tf_op jit(solution)/shard_map/ppermute | solution.py:383
  32.7 0.9 %collective-permute-done.7.their_ref = f32[128,128]{1,0:T(8,128)S(1)} collective-permute-done((f32[128,128]{1,0:T(8,128)S(1)}, f32[128,128]{1,0:T(8,128)S(1)}, u32[]{:S(2)}, u32[]{:S(2)}) %collective-permute-start.7) | collective-permute-done | bytes 65568 | tf_op jit(solution)/shard_map/ppermute | solution.py:383
  33.6 3.0 %linear.1 = (f32[1024,2048]{1,0:T(8,128)S(1)}, f32[8,1,128]{2,1,0:T(1,128)S(1)}) custom-call(bf16[8,2048,256]{2,1,0:T(8,128)(2,1)S(1)} %get-tuple-element.106.fq_ref, f32[1024,2048]{1,0:T(8,128)S(1)} %get-tuple-element.107.part_ref, f32[2,8,128,128]{3,2,1,0:T(8,128)S(1)} %get-tuple-element.108.inner_ref, f32[128,128]{1,0:T(8,128)S(1)} %add.19.mine_ref, ...), custom_call_target="tpu_custom_call" | custom-call | tf_op jit(solution)/shard_map/linear/pallas_call | solution.py:304
  36.7 0.0 copy-start
  36.7 4.1 %collective-permute-start.11 = (f32[8,1,128]{2,1,0:T(1,128)S(1)}, f32[8,1,128]{2,1,0:T(1,128)S(1)}, u32[]{:S(2)}, u32[]{:S(2)}) collective-permute-start(f32[8,1,128]{2,1,0:T(1,128)S(1)} %get-tuple-element.118.s0), channel_id=1, source_target_pairs={{0,3},{1,0},{2,1},{3,2},{4,7},{5,4},{6,5},{7,6},{8,11},{9,8},{10,9... | collective-permute-start | bytes 12296 | tf_op jit(solution)/shard_map/ppermute | solution.py:416
  40.8 0.0 collective-permute-start.10
  40.8 1.3 %collective-permute-start.9 = (f32[8,1,128]{2,1,0:T(1,128)S(1)}, f32[8,1,128]{2,1,0:T(1,128)S(1)}, u32[]{:S(2)}, u32[]{:S(2)}) collective-permute-start(f32[8,1,128]{2,1,0:T(1,128)S(1)} %get-tuple-element.118.s0), channel_id=1, source_target_pairs={{0,1},{1,2},{2,3},{3,0},{4,5},{5,6},{6,7},{7,4},{8,9},{9,10},{10,1... | collective-permute-start | bytes 12296 | tf_op jit(solution)/shard_map/ppermute | solution.py:416
  42.0 0.0 collective-permute-done.8.refs_3_
  42.0 3.3 %shard_map.52.win_ref = f32[1024,2048]{1,0:T(8,128)S(1)} custom-call(f32[256,2048]{1,0:T(8,128)S(1)} %get-tuple-element.115.refs_0_, bf16[2,1024,512]{2,1,0:T(8,128)(2,1)S(1)} %get-tuple-element.62.refs_1_, bf16[2,1024,256]{2,1,0:T(8,128)(2,1)S(1)} %get-tuple-element.63.refs_2_, ...), custom_call_target="tpu_custom_call", output_to_operand_aliasing={{}: (4, {})} | custom-call | tf_op jit(solution)/shard_map/pallas_call | solution.py:268
  45.4 0.0 collective-permute-done.11.s3
  45.4 0.5 %collective-permute-done.10.s2 = f32[8,1,128]{2,1,0:T(1,128)S(1)} collective-permute-done((f32[8,1,128]{2,1,0:T(1,128)S(1)}, f32[8,1,128]{2,1,0:T(1,128)S(1)}, u32[]{:S(2)}, u32[]{:S(2)}) %collective-permute-start.10) | collective-permute-done | bytes 4128 | tf_op jit(solution)/shard_map/ppermute | solution.py:416
  45.9 0.0 collective-permute-done.9.s1
  45.9 0.0 copy-done
  45.9 3.6 %combine.1 = f32[1024,2048]{1,0:T(8,128)} custom-call(f32[1024,2048]{1,0:T(8,128)S(1)} %get-tuple-element.113.lin_ref, f32[1024,2048]{1,0:T(8,128)S(1)} %shard_map.52.win_ref, f32[8,1,128]{2,1,0:T(1,128)S(1)} %get-tuple-element.118.s0, f32[8,1,128]{2,1,0:T(1,128)S(1)} %collective-permute-done.9.s1, f32[8,1,128]{2,1,0:T(1,128)S(1)} %collective-permute-done.10.s2, ...), custom_call_target="tpu_custom_call" | custom-call | tf_op jit(solution)/shard_map/combine/pallas_call | solution.py:347
  (5 shorter events, 0.1 us)
Async XLA Ops:
  2.1 1.4 %collective-permute-start = (f32[2,128,128]{2,1,0:T(8,128)S(1)}, f32[2,128,128]{2,1,0:T(8,128)S(1)}, u32[]{:S(2)}, u32[]{:S(2)}) collective-permute-start(f32[2,128,128]{2,1,0:T(8,128)S(1)} %get-tuple-element.68.own_ref), channel_id=1, source_target_pairs={{0,4},{4,0},{8,12},{12,8},{16,20},{20,16},{24,28},{28,24},{32,36},... | collective-permute-start | bytes 393224 | tf_op jit(solution)/shard_map/ppermute | solution.py:383
  3.5 9.9 %collective-permute-start.3 = (f32[128,128]{1,0:T(8,128)S(1)}, f32[128,128]{1,0:T(8,128)S(1)}, u32[]{:S(2)}, u32[]{:S(2)}) collective-permute-start(f32[128,128]{1,0:T(8,128)S(1)} %shard_map.47.own_ref), channel_id=1, source_target_pairs={{0,24},{4,28},{8,0},{12,4},{16,8},{20,12},{24,16},{28,20},{32,56},... | collective-permute-start | bytes 196616 | tf_op jit(solution)/shard_map/ppermute | solution.py:383
  6.4 7.0 %collective-permute-start.2 = (f32[128,128]{1,0:T(8,128)S(1)}, f32[128,128]{1,0:T(8,128)S(1)}, u32[]{:S(2)}, u32[]{:S(2)}) collective-permute-start(f32[128,128]{1,0:T(8,128)S(1)} %shard_map.47.own_ref), channel_id=1, source_target_pairs={{0,16},{4,20},{8,24},{12,28},{16,0},{20,4},{24,8},{28,12},{32,48},... | collective-permute-start | bytes 196616 | tf_op jit(solution)/shard_map/ppermute | solution.py:383
  7.2 6.3 %collective-permute-start.1 = (f32[128,128]{1,0:T(8,128)S(1)}, f32[128,128]{1,0:T(8,128)S(1)}, u32[]{:S(2)}, u32[]{:S(2)}) collective-permute-start(f32[128,128]{1,0:T(8,128)S(1)} %shard_map.47.own_ref), channel_id=1, source_target_pairs={{0,8},{4,12},{8,16},{12,20},{16,24},{20,28},{24,0},{28,4},{32,40},... | collective-permute-start | bytes 196616 | tf_op jit(solution)/shard_map/ppermute | solution.py:383
  13.5 4.4 %collective-permute-start.4 = (f32[128,128]{1,0:T(8,128)S(1)}, f32[128,128]{1,0:T(8,128)S(1)}, u32[]{:S(2)}, u32[]{:S(2)}) collective-permute-start(f32[128,128]{1,0:T(8,128)S(1)} %get-tuple-element.83), channel_id=1, source_target_pairs={{0,32},{4,36},{8,40},{12,44},{16,48},{20,52},{24,56},{28,60},{1,33... | collective-permute-start | bytes 196616 | tf_op jit(solution)/shard_map/ppermute | solution.py:383
  18.0 4.6 %collective-permute-start.5 = (f32[128,128]{1,0:T(8,128)S(1)}, f32[128,128]{1,0:T(8,128)S(1)}, u32[]{:S(2)}, u32[]{:S(2)}) collective-permute-start(f32[128,128]{1,0:T(8,128)S(1)} %get-tuple-element.121), channel_id=1, source_target_pairs={{32,64},{36,68},{40,72},{44,76},{48,80},{52,84},{56,88},{60,92},{3... | collective-permute-start | bytes 196616 | tf_op jit(solution)/shard_map/ppermute | solution.py:383
  22.6 6.2 %collective-permute-start.6 = (f32[128,128]{1,0:T(8,128)S(1)}, f32[128,128]{1,0:T(8,128)S(1)}, u32[]{:S(2)}, u32[]{:S(2)}) collective-permute-start(f32[128,128]{1,0:T(8,128)S(1)} %get-tuple-element.119), channel_id=1, source_target_pairs={{64,96},{68,100},{72,104},{76,108},{80,112},{84,116},{88,120},{92,... | collective-permute-start | bytes 196616 | tf_op jit(solution)/shard_map/ppermute | solution.py:383
  28.8 13.2 %collective-permute-start.8 = (f32[2,256,128]{2,1,0:T(8,128)S(1)}, f32[2,256,128]{2,1,0:T(8,128)S(1)}, u32[]{:S(2)}, u32[]{:S(2)}) collective-permute-start(f32[2,256,128]{2,1,0:T(8,128)S(1)} %get-tuple-element.116), channel_id=1, source_target_pairs={{0,4},{4,8},{8,12},{12,16},{16,20},{20,24},{24,28},{28,32},{32,36}... | collective-permute-start | bytes 786440 | tf_op jit(solution)/shard_map/ppermute | solution.py:383
  30.7 2.9 %collective-permute-start.7 = (f32[128,128]{1,0:T(8,128)S(1)}, f32[128,128]{1,0:T(8,128)S(1)}, u32[]{:S(2)}, u32[]{:S(2)}) collective-permute-start(f32[128,128]{1,0:T(8,128)S(1)} %add.19.mine_ref), channel_id=1, source_target_pairs={{0,4},{4,0},{8,12},{12,8},{16,20},{20,16},{24,28},{28,24},{32,36},... | collective-permute-start | bytes 196616 | tf_op jit(solution)/shard_map/ppermute | solution.py:383
  36.7 9.2 %copy-start = (f32[2048]{0:T(1024)S(1)}, f32[2048]{0:T(1024)}, u32[]{:S(2)}) copy-start(f32[2048]{0:T(1024)} %param.7) | copy-start | bytes 24580
  36.7 8.7 %collective-permute-start.11 = (f32[8,1,128]{2,1,0:T(1,128)S(1)}, f32[8,1,128]{2,1,0:T(1,128)S(1)}, u32[]{:S(2)}, u32[]{:S(2)}) collective-permute-start(f32[8,1,128]{2,1,0:T(1,128)S(1)} %get-tuple-element.118.s0), channel_id=1, source_target_pairs={{0,3},{1,0},{2,1},{3,2},{4,7},{5,4},{6,5},{7,6},{8,11},{9,8},{10,9... | collective-permute-start | bytes 12296 | tf_op jit(solution)/shard_map/ppermute | solution.py:416
  40.8 5.1 %collective-permute-start.10 = (f32[8,1,128]{2,1,0:T(1,128)S(1)}, f32[8,1,128]{2,1,0:T(1,128)S(1)}, u32[]{:S(2)}, u32[]{:S(2)}) collective-permute-start(f32[8,1,128]{2,1,0:T(1,128)S(1)} %get-tuple-element.118.s0), channel_id=1, source_target_pairs={{0,2},{1,3},{2,0},{3,1},{4,6},{5,7},{6,4},{7,5},{8,10},{9,11},{10,... | collective-permute-start | bytes 12296 | tf_op jit(solution)/shard_map/ppermute | solution.py:416
  40.8 5.1 %collective-permute-start.9 = (f32[8,1,128]{2,1,0:T(1,128)S(1)}, f32[8,1,128]{2,1,0:T(1,128)S(1)}, u32[]{:S(2)}, u32[]{:S(2)}) collective-permute-start(f32[8,1,128]{2,1,0:T(1,128)S(1)} %get-tuple-element.118.s0), channel_id=1, source_target_pairs={{0,1},{1,2},{2,3},{3,0},{4,5},{5,6},{6,7},{7,4},{8,9},{9,10},{10,1... | collective-permute-start | bytes 12296 | tf_op jit(solution)/shard_map/ppermute | solution.py:416
where the time goes:
time: 49.8 us; the launch traced here: 49.6 us
  Pallas kernels  26.4 us (53%)
  starting transfers between devices  16.7 us (34%)
  waiting for transfers between devices  6.11 us (12%)
    pallas_call x5, Pallas kernels, block_part(): pl.pallas_call(lambda *refs: block_body(piece, ahead, len(made), inner, w...  16.1 us
    ppermute x9, starting transfers between devices, move(): return lax.ppermute(x, 'seq', pairs)  11.3 us
    ppermute x9, waiting for transfers between devices, move(): return lax.ppermute(x, 'seq', pairs)  5.58 us
    ppermute x3, starting transfers between devices, shards(): lax.ppermute(sq, 'head', [(i, (i + by) % heads) for i in range(heads)])  5.37 us
    pallas_call x1, Pallas kernels, combine(): pl.pallas_call(combine_body, grid=(1,), in_specs=[pl.BlockSpec(x.shape, l...  3.57 us
    pallas_call x1, Pallas kernels, linear_part(): pl.pallas_call(linear_body, grid=(nb // WIDE,), in_specs=[pl.BlockSpec((W...  3.03 us
    pallas_call x1, Pallas kernels, local_states(): pl.pallas_call(state_body, grid=(kv,), in_specs=[pl.BlockSpec((count, D),...  2.09 us
    pallas_call x1, Pallas kernels, first_queries(): pl.pallas_call(functools.partial(fetch_body, piece), in_specs=[pl.BlockSp...  1.56 us
  transfers between devices with their start and end apart: 12, of which 4 were waited for; matrix products, arithmetic and copies ran while one was open for 0% of the time, Pallas kernels for 42%

commit v1 on v0

--- a/solution.py
+++ b/solution.py
@@ -15,7 +15,7 @@
 G = QUERY_HEADS // KEY_VALUE_HEADS
 BLOCK = 128
 STEP = 2
-WIDE = 4
+WIDE = 8
 EPS = 1e-6
 SCORE_SCALE = math.log2(math.e) / math.sqrt(D)
 
@@ -218,6 +218,7 @@
         for i, at in enumerate(heads):
             win_ref[tokens, at] = win[i * BLOCK : (i + 1) * BLOCK]
 
+    waiting = None
     for j in range(STEP):
         block = piece * STEP + j
         tokens = slice(j * BLOCK, (j + 1) * BLOCK)
@@ -227,11 +228,17 @@
             heads = [slice(i * D, (i + 1) * D) for i in range(g * G, (g + 1) * G)]
             q = rows(*[q_ref[tokens, at] for at in heads])
             if window:
-                s, v_both = scores(block, g, q, here, there)
+                made = (block, *scores(block, g, q, here, there), heads, tokens)
             if inner:
                 in_block(j, g, q, heads, tokens, here)
-            if window:
-                in_window(block, s, v_both, heads, tokens)
+                if window:
+                    in_window(*made)
+            else:
+                if waiting is not None:
+                    in_window(*waiting)
+                waiting = made
+    if waiting is not None:
+        in_window(*waiting)
     if ahead is not None:
         for j in range(STEP):
             fetch(j).wait()

time: 49.8 us -> 49.5 us (level)
  Pallas kernels: 26.4 us -> 25.2 us
  waiting for transfers between devices: 6.11 us -> 7.01 us
    pallas_call x5, Pallas kernels: 16.1 us -> 15.2 us  [block_part(): pl.pallas_call(lambda *refs: block_body(piece, ahead, len(made), inner, w...]
    ppermute x3, waiting for transfers between devices: 0.52 us -> 1.43 us  [shards(): lax.ppermute(sq, 'head', [(i, (i + by) % heads) for i in range(heads)])]
  transfers between devices with their start and end apart: 12 -> 12, of which waited for: 4 -> 4; matrix products, arithmetic and copies ran while one was open for 0% -> 0% of each run, Pallas kernels for 42% -> 40%
where the time goes in v1:
time: 49.5 us; the launch traced here: 49.2 us
  Pallas kernels  25.2 us (51%)
  starting transfers between devices  16.7 us (34%)
  waiting for transfers between devices  7.01 us (14%)
    pallas_call x5, Pallas kernels, block_part(): pl.pallas_call(lambda *refs: block_body(piece, ahead, len(made), inner, w...  15.2 us
    ppermute x9, starting transfers between devices, move(): return lax.ppermute(x, 'seq', pairs)  11.3 us
    ppermute x9, waiting for transfers between devices, move(): return lax.ppermute(x, 'seq', pairs)  5.58 us
    ppermute x3, starting transfers between devices, shards(): lax.ppermute(sq, 'head', [(i, (i + by) % heads) for i in range(heads)])  5.37 us
    pallas_call x1, Pallas kernels, combine(): pl.pallas_call(combine_body, grid=(1,), in_specs=[pl.BlockSpec(x.shape, l...  3.57 us
    pallas_call x1, Pallas kernels, linear_part(): pl.pallas_call(linear_body, grid=(nb // WIDE,), in_specs=[pl.BlockSpec((W...  2.67 us
    pallas_call x1, Pallas kernels, local_states(): pl.pallas_call(state_body, grid=(kv,), in_specs=[pl.BlockSpec((count, D),...  2.09 us
    pallas_call x1, Pallas kernels, first_queries(): pl.pallas_call(functools.partial(fetch_body, piece), in_specs=[pl.BlockSp...  1.56 us
  transfers between devices with their start and end apart: 12, of which 4 were waited for; matrix products, arithmetic and copies ran while one was open for 0% of the time, Pallas kernels for 40%

profile of v1, /device:TPU:24, one launch (start us, length us, event | category | flops | bytes accessed | tf_op | source)
XLA Modules:
  0.0 49.2 jit_solution(6575036563515981801)
XLA Ops:
  0.0 2.1 %local_states.1 = (f32[2,8,128,128]{3,2,1,0:T(8,128)S(1)}, f32[2,128,128]{2,1,0:T(8,128)S(1)}, f32[2,256,128]{2,1,0:T(8,128)S(1)}, bf16[2,1024,512]{2,1,0:T(8,128)(2,1)S(1)}, bf16[2,1024,256]{2,1,0:T(8,128)(2,1)S(1)}) custom-call(f32[1024,256]{1,0:T(8,128)} %k_ref.1, f32[1024,256]{1,0:T(8,128)} %v_ref.1), custom_call_target="tpu_custom_call" | custom-call | tf_op jit(solution)/shard_map/local_states/pallas_call | solution.py:77
  2.1 0.1 collective-permute-start
  2.2 1.3 %collective-permute-done.other_ref = f32[2,128,128]{2,1,0:T(8,128)S(1)} collective-permute-done((f32[2,128,128]{2,1,0:T(8,128)S(1)}, f32[2,128,128]{2,1,0:T(8,128)S(1)}, u32[]{:S(2)}, u32[]{:S(2)}) %collective-permute-start) | collective-permute-done | bytes 131104 | tf_op jit(solution)/shard_map/ppermute | solution.py:390
  3.5 2.8 %collective-permute-start.3 = (f32[128,128]{1,0:T(8,128)S(1)}, f32[128,128]{1,0:T(8,128)S(1)}, u32[]{:S(2)}, u32[]{:S(2)}) collective-permute-start(f32[128,128]{1,0:T(8,128)S(1)} %shard_map.47.own_ref), channel_id=1, source_target_pairs={{0,24},{4,28},{8,0},{12,4},{16,8},{20,12},{24,16},{28,20},{32,56},... | collective-permute-start | bytes 196616 | tf_op jit(solution)/shard_map/ppermute | solution.py:390
  6.4 0.8 %collective-permute-start.2 = (f32[128,128]{1,0:T(8,128)S(1)}, f32[128,128]{1,0:T(8,128)S(1)}, u32[]{:S(2)}, u32[]{:S(2)}) collective-permute-start(f32[128,128]{1,0:T(8,128)S(1)} %shard_map.47.own_ref), channel_id=1, source_target_pairs={{0,16},{4,20},{8,24},{12,28},{16,0},{20,4},{24,8},{28,12},{32,48},... | collective-permute-start | bytes 196616 | tf_op jit(solution)/shard_map/ppermute | solution.py:390
  7.2 0.9 %collective-permute-start.1 = (f32[128,128]{1,0:T(8,128)S(1)}, f32[128,128]{1,0:T(8,128)S(1)}, u32[]{:S(2)}, u32[]{:S(2)}) collective-permute-start(f32[128,128]{1,0:T(8,128)S(1)} %shard_map.47.own_ref), channel_id=1, source_target_pairs={{0,8},{4,12},{8,16},{12,20},{16,24},{20,28},{24,0},{28,4},{32,40},... | collective-permute-start | bytes 196616 | tf_op jit(solution)/shard_map/ppermute | solution.py:390
  8.1 1.6 %first_queries.1.refs_0_ = f32[256,2048]{1,0:T(8,128)S(1)} custom-call(f32[1024,2048]{1,0:T(8,128)} %refs_3_.5), custom_call_target="tpu_custom_call" | custom-call | tf_op jit(solution)/shard_map/first_queries/pallas_call | solution.py:114
  9.6 3.8 %shard_map.46 = (f32[1024,2048]{1,0:T(8,128)S(1)}, f32[1024,2048]{1,0:T(8,128)S(1)}, bf16[8,2048,256]{2,1,0:T(8,128)(2,1)S(1)}, f32[256,2048]{1,0:T(8,128)S(1)}) custom-call(f32[256,2048]{1,0:T(8,128)S(1)} %first_queries.1.refs_0_, bf16[2,1024,512]{2,1,0:T(8,128)(2,1)S(1)} %get-tuple-element.62.refs_1_, bf16[2,1024,256]{2,1,0:T(8,128)(2,1)S(1)} %get-tuple-element.63.refs_2_, ...), custom_call_target="tpu_custom_call" | custom-call | tf_op jit(solution)/shard_map/pallas_call | solution.py:275
  13.4 0.0 collective-permute-done.3.three_ref
  13.4 0.0 collective-permute-done.2.two_ref
  13.4 0.0 collective-permute-done.1.one_ref
  13.5 0.7 %collective-permute-start.4 = (f32[128,128]{1,0:T(8,128)S(1)}, f32[128,128]{1,0:T(8,128)S(1)}, u32[]{:S(2)}, u32[]{:S(2)}) collective-permute-start(f32[128,128]{1,0:T(8,128)S(1)} %get-tuple-element.83), channel_id=1, source_target_pairs={{0,32},{4,36},{8,40},{12,44},{16,48},{20,52},{24,56},{28,60},{1,33... | collective-permute-start | bytes 196616 | tf_op jit(solution)/shard_map/ppermute | solution.py:390
  14.2 3.8 %shard_map.49 = (f32[1024,2048]{1,0:T(8,128)S(1)}, f32[1024,2048]{1,0:T(8,128)S(1)}, bf16[8,2048,256]{2,1,0:T(8,128)(2,1)S(1)}, f32[256,2048]{1,0:T(8,128)S(1)}) custom-call(f32[256,2048]{1,0:T(8,128)S(1)} %get-tuple-element.64.refs_0_, ...), custom_call_target="tpu_custom_call", output_to_operand_aliasing={{0}: (4, {}), {1}: (5, {}), {2}: (6, {})} | custom-call | tf_op jit(solution)/shard_map/pallas_call | solution.py:275
  17.9 0.0 collective-permute-done.4
  18.0 0.8 %collective-permute-start.5 = (f32[128,128]{1,0:T(8,128)S(1)}, f32[128,128]{1,0:T(8,128)S(1)}, u32[]{:S(2)}, u32[]{:S(2)}) collective-permute-start(f32[128,128]{1,0:T(8,128)S(1)} %get-tuple-element.121), channel_id=1, source_target_pairs={{32,64},{36,68},{40,72},{44,76},{48,80},{52,84},{56,88},{60,92},{3... | collective-permute-start | bytes 196616 | tf_op jit(solution)/shard_map/ppermute | solution.py:390
  18.8 3.8 %shard_map.50 = (f32[1024,2048]{1,0:T(8,128)S(1)}, f32[1024,2048]{1,0:T(8,128)S(1)}, bf16[8,2048,256]{2,1,0:T(8,128)(2,1)S(1)}, f32[256,2048]{1,0:T(8,128)S(1)}) custom-call(f32[256,2048]{1,0:T(8,128)S(1)} %get-tuple-element.79.refs_0_, ...), custom_call_target="tpu_custom_call", output_to_operand_aliasing={{0}: (4, {}), {1}: (5, {}), {2}: (6, {})} | custom-call | tf_op jit(solution)/shard_map/pallas_call | solution.py:275
  22.6 0.0 collective-permute-done.5
  22.6 1.3 %collective-permute-start.6 = (f32[128,128]{1,0:T(8,128)S(1)}, f32[128,128]{1,0:T(8,128)S(1)}, u32[]{:S(2)}, u32[]{:S(2)}) collective-permute-start(f32[128,128]{1,0:T(8,128)S(1)} %get-tuple-element.119), channel_id=1, source_target_pairs={{64,96},{68,100},{72,104},{76,108},{80,112},{84,116},{88,120},{92,... | collective-permute-start | bytes 196616 | tf_op jit(solution)/shard_map/ppermute | solution.py:390
  23.9 1.5 %shard_map.51 = (f32[1024,2048]{1,0:T(8,128)S(1)}, bf16[8,2048,256]{2,1,0:T(8,128)(2,1)S(1)}) custom-call(f32[256,2048]{1,0:T(8,128)S(1)} %get-tuple-element.115.refs_0_, bf16[2,1024,512]{2,1,0:T(8,128)(2,1)S(1)} %get-tuple-element.62.refs_1_, bf16[2,1024,256]{2,1,0:T(8,128)(2,1)S(1)} %get-tuple-element.63.refs_2_, ...), custom_call_target="tpu_custom_call", output_to_operand_aliasing={{0}: (3, {}), {1}: (4, {})} | custom-call | tf_op jit(solution)/shard_map/pallas_call | solution.py:275
  25.5 3.3 %collective-permute-done.6 = f32[128,128]{1,0:T(8,128)S(1)} collective-permute-done((f32[128,128]{1,0:T(8,128)S(1)}, f32[128,128]{1,0:T(8,128)S(1)}, u32[]{:S(2)}, u32[]{:S(2)}) %collective-permute-start.6) | collective-permute-done | bytes 65568 | tf_op jit(solution)/shard_map/ppermute | solution.py:390
  28.8 1.9 %collective-permute-start.8 = (f32[2,256,128]{2,1,0:T(8,128)S(1)}, f32[2,256,128]{2,1,0:T(8,128)S(1)}, u32[]{:S(2)}, u32[]{:S(2)}) collective-permute-start(f32[2,256,128]{2,1,0:T(8,128)S(1)} %get-tuple-element.116), channel_id=1, source_target_pairs={{0,4},{4,8},{8,12},{12,16},{16,20},{20,24},{24,28},{28,32},{32,36}... | collective-permute-start | bytes 786440 | tf_op jit(solution)/shard_map/ppermute | solution.py:390
  30.7 2.0 %collective-permute-start.7 = (f32[128,128]{1,0:T(8,128)S(1)}, f32[128,128]{1,0:T(8,128)S(1)}, u32[]{:S(2)}, u32[]{:S(2)}) collective-permute-start(f32[128,128]{1,0:T(8,128)S(1)} %add.19.mine_ref), channel_id=1, source_target_pairs={{0,4},{4,0},{8,12},{12,8},{16,20},{20,16},{24,28},{28,24},{32,36},... | collective-permute-start | bytes 196616 | tf_op jit(solution)/shard_map/ppermute | solution.py:390
  32.7 0.9 %collective-permute-done.7.their_ref = f32[128,128]{1,0:T(8,128)S(1)} collective-permute-done((f32[128,128]{1,0:T(8,128)S(1)}, f32[128,128]{1,0:T(8,128)S(1)}, u32[]{:S(2)}, u32[]{:S(2)}) %collective-permute-start.7) | collective-permute-done | bytes 65568 | tf_op jit(solution)/shard_map/ppermute | solution.py:390
  33.6 2.7 %linear.1 = (f32[1024,2048]{1,0:T(8,128)S(1)}, f32[8,1,128]{2,1,0:T(1,128)S(1)}) custom-call(bf16[8,2048,256]{2,1,0:T(8,128)(2,1)S(1)} %get-tuple-element.106.fq_ref, f32[1024,2048]{1,0:T(8,128)S(1)} %get-tuple-element.107.part_ref, f32[2,8,128,128]{3,2,1,0:T(8,128)S(1)} %get-tuple-element.108.inner_ref, f32[128,128]{1,0:T(8,128)S(1)} %add.19.mine_ref, ...), custom_call_target="tpu_custom_call" | custom-call | tf_op jit(solution)/shard_map/linear/pallas_call | solution.py:311
  36.3 0.0 copy-start
  36.3 4.1 %collective-permute-start.11 = (f32[8,1,128]{2,1,0:T(1,128)S(1)}, f32[8,1,128]{2,1,0:T(1,128)S(1)}, u32[]{:S(2)}, u32[]{:S(2)}) collective-permute-start(f32[8,1,128]{2,1,0:T(1,128)S(1)} %get-tuple-element.118.s0), channel_id=1, source_target_pairs={{0,3},{1,0},{2,1},{3,2},{4,7},{5,4},{6,5},{7,6},{8,11},{9,8},{10,9... | collective-permute-start | bytes 12296 | tf_op jit(solution)/shard_map/ppermute | solution.py:423
  40.4 0.0 collective-permute-start.10
  40.4 1.3 %collective-permute-start.9 = (f32[8,1,128]{2,1,0:T(1,128)S(1)}, f32[8,1,128]{2,1,0:T(1,128)S(1)}, u32[]{:S(2)}, u32[]{:S(2)}) collective-permute-start(f32[8,1,128]{2,1,0:T(1,128)S(1)} %get-tuple-element.118.s0), channel_id=1, source_target_pairs={{0,1},{1,2},{2,3},{3,0},{4,5},{5,6},{6,7},{7,4},{8,9},{9,10},{10,1... | collective-permute-start | bytes 12296 | tf_op jit(solution)/shard_map/ppermute | solution.py:423
  41.7 0.0 collective-permute-done.8.refs_3_
  41.7 2.4 %shard_map.52.win_ref = f32[1024,2048]{1,0:T(8,128)S(1)} custom-call(f32[256,2048]{1,0:T(8,128)S(1)} %get-tuple-element.115.refs_0_, bf16[2,1024,512]{2,1,0:T(8,128)(2,1)S(1)} %get-tuple-element.62.refs_1_, bf16[2,1024,256]{2,1,0:T(8,128)(2,1)S(1)} %get-tuple-element.63.refs_2_, ...), custom_call_target="tpu_custom_call", output_to_operand_aliasing={{}: (4, {})} | custom-call | tf_op jit(solution)/shard_map/pallas_call | solution.py:275
  44.1 0.0 collective-permute-done.11.s3
  44.1 1.4 %collective-permute-done.10.s2 = f32[8,1,128]{2,1,0:T(1,128)S(1)} collective-permute-done((f32[8,1,128]{2,1,0:T(1,128)S(1)}, f32[8,1,128]{2,1,0:T(1,128)S(1)}, u32[]{:S(2)}, u32[]{:S(2)}) %collective-permute-start.10) | collective-permute-done | bytes 4128 | tf_op jit(solution)/shard_map/ppermute | solution.py:423
  45.5 0.0 collective-permute-done.9.s1
  45.5 0.0 copy-done
  45.5 3.6 %combine.1 = f32[1024,2048]{1,0:T(8,128)} custom-call(f32[1024,2048]{1,0:T(8,128)S(1)} %get-tuple-element.113.lin_ref, f32[1024,2048]{1,0:T(8,128)S(1)} %shard_map.52.win_ref, f32[8,1,128]{2,1,0:T(1,128)S(1)} %get-tuple-element.118.s0, f32[8,1,128]{2,1,0:T(1,128)S(1)} %collective-permute-done.9.s1, f32[8,1,128]{2,1,0:T(1,128)S(1)} %collective-permute-done.10.s2, ...), custom_call_target="tpu_custom_call" | custom-call | tf_op jit(solution)/shard_map/combine/pallas_call | solution.py:354
  (5 shorter events, 0.1 us)
Async XLA Ops:
  2.1 1.4 %collective-permute-start = (f32[2,128,128]{2,1,0:T(8,128)S(1)}, f32[2,128,128]{2,1,0:T(8,128)S(1)}, u32[]{:S(2)}, u32[]{:S(2)}) collective-permute-start(f32[2,128,128]{2,1,0:T(8,128)S(1)} %get-tuple-element.68.own_ref), channel_id=1, source_target_pairs={{0,4},{4,0},{8,12},{12,8},{16,20},{20,16},{24,28},{28,24},{32,36},... | collective-permute-start | bytes 393224 | tf_op jit(solution)/shard_map/ppermute | solution.py:390
  3.5 9.9 %collective-permute-start.3 = (f32[128,128]{1,0:T(8,128)S(1)}, f32[128,128]{1,0:T(8,128)S(1)}, u32[]{:S(2)}, u32[]{:S(2)}) collective-permute-start(f32[128,128]{1,0:T(8,128)S(1)} %shard_map.47.own_ref), channel_id=1, source_target_pairs={{0,24},{4,28},{8,0},{12,4},{16,8},{20,12},{24,16},{28,20},{32,56},... | collective-permute-start | bytes 196616 | tf_op jit(solution)/shard_map/ppermute | solution.py:390
  6.4 7.0 %collective-permute-start.2 = (f32[128,128]{1,0:T(8,128)S(1)}, f32[128,128]{1,0:T(8,128)S(1)}, u32[]{:S(2)}, u32[]{:S(2)}) collective-permute-start(f32[128,128]{1,0:T(8,128)S(1)} %shard_map.47.own_ref), channel_id=1, source_target_pairs={{0,16},{4,20},{8,24},{12,28},{16,0},{20,4},{24,8},{28,12},{32,48},... | collective-permute-start | bytes 196616 | tf_op jit(solution)/shard_map/ppermute | solution.py:390
  7.2 6.3 %collective-permute-start.1 = (f32[128,128]{1,0:T(8,128)S(1)}, f32[128,128]{1,0:T(8,128)S(1)}, u32[]{:S(2)}, u32[]{:S(2)}) collective-permute-start(f32[128,128]{1,0:T(8,128)S(1)} %shard_map.47.own_ref), channel_id=1, source_target_pairs={{0,8},{4,12},{8,16},{12,20},{16,24},{20,28},{24,0},{28,4},{32,40},... | collective-permute-start | bytes 196616 | tf_op jit(solution)/shard_map/ppermute | solution.py:390
  13.5 4.4 %collective-permute-start.4 = (f32[128,128]{1,0:T(8,128)S(1)}, f32[128,128]{1,0:T(8,128)S(1)}, u32[]{:S(2)}, u32[]{:S(2)}) collective-permute-start(f32[128,128]{1,0:T(8,128)S(1)} %get-tuple-element.83), channel_id=1, source_target_pairs={{0,32},{4,36},{8,40},{12,44},{16,48},{20,52},{24,56},{28,60},{1,33... | collective-permute-start | bytes 196616 | tf_op jit(solution)/shard_map/ppermute | solution.py:390
  18.0 4.6 %collective-permute-start.5 = (f32[128,128]{1,0:T(8,128)S(1)}, f32[128,128]{1,0:T(8,128)S(1)}, u32[]{:S(2)}, u32[]{:S(2)}) collective-permute-start(f32[128,128]{1,0:T(8,128)S(1)} %get-tuple-element.121), channel_id=1, source_target_pairs={{32,64},{36,68},{40,72},{44,76},{48,80},{52,84},{56,88},{60,92},{3... | collective-permute-start | bytes 196616 | tf_op jit(solution)/shard_map/ppermute | solution.py:390
  22.6 6.2 %collective-permute-start.6 = (f32[128,128]{1,0:T(8,128)S(1)}, f32[128,128]{1,0:T(8,128)S(1)}, u32[]{:S(2)}, u32[]{:S(2)}) collective-permute-start(f32[128,128]{1,0:T(8,128)S(1)} %get-tuple-element.119), channel_id=1, source_target_pairs={{64,96},{68,100},{72,104},{76,108},{80,112},{84,116},{88,120},{92,... | collective-permute-start | bytes 196616 | tf_op jit(solution)/shard_map/ppermute | solution.py:390
  28.8 12.9 %collective-permute-start.8 = (f32[2,256,128]{2,1,0:T(8,128)S(1)}, f32[2,256,128]{2,1,0:T(8,128)S(1)}, u32[]{:S(2)}, u32[]{:S(2)}) collective-permute-start(f32[2,256,128]{2,1,0:T(8,128)S(1)} %get-tuple-element.116), channel_id=1, source_target_pairs={{0,4},{4,8},{8,12},{12,16},{16,20},{20,24},{24,28},{28,32},{32,36}... | collective-permute-start | bytes 786440 | tf_op jit(solution)/shard_map/ppermute | solution.py:390
  30.7 2.9 %collective-permute-start.7 = (f32[128,128]{1,0:T(8,128)S(1)}, f32[128,128]{1,0:T(8,128)S(1)}, u32[]{:S(2)}, u32[]{:S(2)}) collective-permute-start(f32[128,128]{1,0:T(8,128)S(1)} %add.19.mine_ref), channel_id=1, source_target_pairs={{0,4},{4,0},{8,12},{12,8},{16,20},{20,16},{24,28},{28,24},{32,36},... | collective-permute-start | bytes 196616 | tf_op jit(solution)/shard_map/ppermute | solution.py:390
  36.3 9.2 %copy-start = (f32[2048]{0:T(1024)S(1)}, f32[2048]{0:T(1024)}, u32[]{:S(2)}) copy-start(f32[2048]{0:T(1024)} %param.7) | copy-start | bytes 24580
  36.3 7.8 %collective-permute-start.11 = (f32[8,1,128]{2,1,0:T(1,128)S(1)}, f32[8,1,128]{2,1,0:T(1,128)S(1)}, u32[]{:S(2)}, u32[]{:S(2)}) collective-permute-start(f32[8,1,128]{2,1,0:T(1,128)S(1)} %get-tuple-element.118.s0), channel_id=1, source_target_pairs={{0,3},{1,0},{2,1},{3,2},{4,7},{5,4},{6,5},{7,6},{8,11},{9,8},{10,9... | collective-permute-start | bytes 12296 | tf_op jit(solution)/shard_map/ppermute | solution.py:423
  40.4 5.1 %collective-permute-start.10 = (f32[8,1,128]{2,1,0:T(1,128)S(1)}, f32[8,1,128]{2,1,0:T(1,128)S(1)}, u32[]{:S(2)}, u32[]{:S(2)}) collective-permute-start(f32[8,1,128]{2,1,0:T(1,128)S(1)} %get-tuple-element.118.s0), channel_id=1, source_target_pairs={{0,2},{1,3},{2,0},{3,1},{4,6},{5,7},{6,4},{7,5},{8,10},{9,11},{10,... | collective-permute-start | bytes 12296 | tf_op jit(solution)/shard_map/ppermute | solution.py:423
  40.4 5.1 %collective-permute-start.9 = (f32[8,1,128]{2,1,0:T(1,128)S(1)}, f32[8,1,128]{2,1,0:T(1,128)S(1)}, u32[]{:S(2)}, u32[]{:S(2)}) collective-permute-start(f32[8,1,128]{2,1,0:T(1,128)S(1)} %get-tuple-element.118.s0), channel_id=1, source_target_pairs={{0,1},{1,2},{2,3},{3,0},{4,5},{5,6},{6,7},{7,4},{8,9},{9,10},{10,1... | collective-permute-start | bytes 12296 | tf_op jit(solution)/shard_map/ppermute | solution.py:423
